TPU v7x, 512 devices: a whole 4x8x8 slice. The times are simulated.
512 devices in a mesh: rows: 64 (over y, x, core), cols: 8 (over z).
Axes of the slice: x: 4, y: 8, z: 8, core: 2. Of those that a mesh axis runs over, the one named last changes fastest.
Arguments:
- fact_cells: bfloat16 [3072, 32, 512], P('rows', 'cols'), may hold values from -6 to 6
- gain_col: float32 [512], replicated, may hold values from 0.1 to 1.9
- w_qkv: bfloat16 [512, 1536], replicated, may hold values from -0.25 to 0.25
- w_col_out: bfloat16 [512, 512], replicated, may hold values from -0.25 to 0.25
- gain_tile: float32 [512], replicated, may hold values from 0.1 to 1.9
- w_query: bfloat16 [512, 512], replicated, may hold values from -0.25 to 0.25
- w_tile_out: bfloat16 [512, 512], replicated, may hold values from -0.25 to 0.25
- tile_kv: bfloat16 [256, 128, 8, 128], P('rows', None, 'cols'), may hold values from -70 to 70
- tile_ids: int32 [64, 48], P('rows'), may hold values from -1 to 255, as said below
- key_mask: int32 [3072, 48], P('rows'), may hold values from 0 to 1, as said below
Outputs:
- layer_out: bfloat16 [3072, 32, 512], P('rows', 'cols')
Inputs may be any that keep to these rules, and one draw needn't show every extreme that they name: `tile_ids`: tile t is held by index t // 4 of rows. In every block the first slots, 36 of them or more, hold distinct tile ids and the rest hold -1; some block fills all 48 slots. The listed tiles of one block are held by distinct indices of rows. `key_mask`: 0 wherever the row's block holds -1 in that slot; 1 in slot 0 of every row.
All inputs are finite; a program needn't handle non-finite values.
Results may differ from a plain program's by a relative error of at most 0.023.
The roundings to bfloat16 on the way count: a program that leaves them out, or rounds other values in their place, can miss the bound.
Values may be sent and summed in bfloat16 or wider, within the bound.
A program may use at most 64 MiB of HBM per device.

v0:
```python
import jax
import jax.numpy as jnp
from jax import lax
from jax.sharding import PartitionSpec as P


def rms_scale(values, gain_vec):
    mean_sq = jnp.mean(values * values, axis=-1, keepdims=True)
    return values * lax.rsqrt(mean_sq + 1e-05) * gain_vec


def soft_weights(scores, axes):
    row_top = jnp.max(scores, axis=axes, keepdims=True)
    expo_vals = jnp.exp(scores - row_top)
    return (expo_vals / jnp.sum(expo_vals, axis=axes, keepdims=True)).astype(jnp.bfloat16)


def column_attend(queries, keyvals, head_size):
    key_part = keyvals[..., :head_size]
    val_part = keyvals[..., head_size:]
    scores = jnp.einsum(
        "rchd,rkhd->rhck", queries, key_part, preferred_element_type=jnp.float32
    ) * head_size ** (-0.5)
    col_weights = soft_weights(scores, (3,))
    return jnp.einsum(
        "rhck,rkhd->rchd", col_weights, val_part, preferred_element_type=jnp.float32
    ).astype(jnp.bfloat16)


def tile_attend(queries, fetched, key_mask, head_size):
    key_part = fetched[..., :head_size]
    val_part = fetched[..., head_size:]
    row_count, col_count, head_count = queries.shape[:3]
    q_blocks = queries.reshape(row_count // 4, 4, col_count, head_count, head_size)
    m_blocks = key_mask.reshape(row_count // 4, 4, key_mask.shape[1])

    def one_block(block_pair):
        block_q, block_m = block_pair
        scores = jnp.einsum(
            "rchd,tkhd->rchtk", block_q, key_part, preferred_element_type=jnp.float32
        ) * head_size ** (-0.5)
        live_keys = (block_m > 0)[:, None, None, :, None]
        scores = jnp.where(live_keys, scores, -1e30)
        tile_weights = soft_weights(scores, (3, 4))
        return jnp.einsum(
            "rchtk,tkhd->rchd", tile_weights, val_part, preferred_element_type=jnp.float32
        ).astype(jnp.bfloat16)

    answer = lax.map(one_block, (q_blocks, m_blocks))
    return answer.reshape(row_count, col_count, head_count, head_size)


def fetch_all(tile_kv, tile_ids):
    gathered = lax.all_gather(tile_kv, "rows", axis=0, tiled=True)
    return jnp.take(gathered, jnp.maximum(tile_ids[0], 0), axis=0)


def project(normed, weight):
    return jnp.dot(normed.reshape(-1, weight.shape[0]), weight, preferred_element_type=jnp.float32)


def shards(
    fact_cells,
    gain_col,
    w_qkv,
    w_col_out,
    gain_tile,
    w_query,
    w_tile_out,
    tile_kv,
    tile_ids,
    key_mask,
):
    model_width = fact_cells.shape[2]
    head_size = tile_kv.shape[3] // 2
    heads_all = model_width // head_size
    fetched = fetch_all(tile_kv, tile_ids)
    row_count, col_local = (fact_cells.shape[0], fact_cells.shape[1])
    residual = fact_cells.astype(jnp.float32)
    normed = rms_scale(residual, gain_col).astype(jnp.bfloat16)
    packed = (
        project(normed, w_qkv)
        .astype(jnp.bfloat16)
        .reshape(row_count, col_local, 3, heads_all, head_size)
    )
    queries = packed[:, :, 0]
    keyvals = jnp.concatenate([packed[:, :, 1], packed[:, :, 2]], axis=-1)
    queries_h, keyvals_h = (
        lax.all_to_all(queries, "cols", split_axis=2, concat_axis=1, tiled=True),
        lax.all_to_all(keyvals, "cols", split_axis=2, concat_axis=1, tiled=True),
    )
    mixed_col = column_attend(queries_h, keyvals_h, head_size)
    mixed_back = lax.all_to_all(mixed_col, "cols", split_axis=1, concat_axis=2, tiled=True)
    residual = residual + project(mixed_back, w_col_out).reshape(residual.shape)
    normed2 = rms_scale(residual, gain_tile).astype(jnp.bfloat16)
    asked_q = (
        project(normed2, w_query)
        .astype(jnp.bfloat16)
        .reshape(row_count, col_local, heads_all, head_size)
    )
    asked_h = lax.all_to_all(asked_q, "cols", split_axis=2, concat_axis=1, tiled=True)
    answer = tile_attend(asked_h, fetched, key_mask, head_size)
    answer_back = lax.all_to_all(answer, "cols", split_axis=1, concat_axis=2, tiled=True)
    final_out = residual + project(answer_back, w_tile_out).reshape(residual.shape)
    return final_out.astype(jnp.bfloat16)


def solution(mesh):
    placed = (
        P("rows", "cols", None),
        P(),
        P(),
        P(),
        P(),
        P(),
        P(),
        P("rows", None, "cols", None),
        P("rows", None),
        P("rows", None),
    )
    return jax.shard_map(
        shards, mesh=mesh, in_specs=placed, out_specs=P("rows", "cols", None), check_vma=False
    )
```

profile of v0, /device:TPU:8, one launch (start us, length us, event | category | flops | bytes accessed | tf_op | source)
XLA Modules:
  0.0 198.4 jit_solution(1383678545264350636)
XLA Ops:
  6.5 0.7 all-gather.2.cloned.1.call-update
  7.3 1.1 fusion.30
  8.3 1.1 fusion.32
  11.1 1.0 reshape.174
  12.1 10.3 %all-to-all-start.1 = ((bf16[8,2,6144]{2,1,0:T(2,128)(2,1)}), bf16[8,2,6144]{2,1,0:T(2,128)(2,1)S(1)}, u32[]{:S(2)}, u32[]{:S(2)}) async-start(bf16[8,2,6144]{2,1,0:T(2,128)(2,1)} %reshape.174), calls=%async_computation.1 | async-start | bytes 393216 | tf_op jit(solution)/shard_map/all_to_all | solution.py:89
  22.8 1.3 pad_maximum_fusion
  24.2 8.8 %all-to-all-done.1 = bf16[8,2,6144]{2,1,0:T(2,128)(2,1)S(1)} async-done(((bf16[8,2,6144]{2,1,0:T(2,128)(2,1)}), bf16[8,2,6144]{2,1,0:T(2,128)(2,1)S(1)}, u32[]{:S(2)}, u32[]{:S(2)}) %all-to-all-start.1) | async-done | bytes 196640 | tf_op jit(solution)/shard_map/all_to_all | solution.py:89
  32.9 3.5 %all-to-all-start = ((bf16[48,4,8,128]{3,1,0,2:T(4,128)(2,1)}), bf16[48,4,8,128]{3,1,0,2:T(4,128)(2,1)S(1)}, u32[]{:S(2)}, u32[]{:S(2)}) async-start(bf16[48,4,8,128]{3,1,0,2:T(4,128)(2,1)} %pad_maximum_fusion), calls=%async_computation | async-start | bytes 786432 | tf_op jit(solution)/shard_map/all_to_all | solution.py:90
  37.0 12.4 %all-to-all-done = bf16[48,4,8,128]{3,1,0,2:T(4,128)(2,1)S(1)} async-done(((bf16[48,4,8,128]{3,1,0,2:T(4,128)(2,1)}), bf16[48,4,8,128]{3,1,0,2:T(4,128)(2,1)S(1)}, u32[]{:S(2)}, u32[]{:S(2)}) %all-to-all-start) | async-done | bytes 393248 | tf_op jit(solution)/shard_map/all_to_all | solution.py:90
  49.5 1.3 fusion.38
  50.8 1.6 fusion.26
  52.9 12.2 %all_to_all.78 = bf16[8,2,6144]{2,1,0:T(2,128)(2,1)S(1)} all-to-all(bf16[8,2,6144]{2,1,0:T(2,128)(2,1)S(1)} %reshape.176), channel_id=1, replica_groups=mesh['rows'=64,'cols'=8] {'cols'}, dimensions={0} | all-to-all | bytes 393216 | tf_op jit(solution)/shard_map/all_to_all | solution.py:93
  66.7 1.3 convolution_convert_fusion.2
  68.4 1.0 reshape.178
  69.3 3.6 %all-to-all-start.3 = ((bf16[8,2,6144]{2,1,0:T(2,128)(2,1)}), bf16[8,2,6144]{2,1,0:T(2,128)(2,1)S(1)}, u32[]{:S(2)}, u32[]{:S(2)}) async-start(bf16[8,2,6144]{2,1,0:T(2,128)(2,1)} %reshape.178), calls=%async_computation.3 | async-start | bytes 393216 | tf_op jit(solution)/shard_map/all_to_all | solution.py:101
  73.0 9.4 %all-to-all-done.3 = bf16[8,2,6144]{2,1,0:T(2,128)(2,1)S(1)} async-done(((bf16[8,2,6144]{2,1,0:T(2,128)(2,1)}), bf16[8,2,6144]{2,1,0:T(2,128)(2,1)S(1)}, u32[]{:S(2)}, u32[]{:S(2)}) %all-to-all-start.3) | async-done | bytes 196640 | tf_op jit(solution)/shard_map/all_to_all | solution.py:101
  82.9 0.9 copy.63
  83.8 20.0 %all-gather.2.cloned.1.call-done = bf16[256,128,1,128]{3,1,2,0:T(8,128)(2,1)} async-done(((bf16[4,128,1,128]{3,1,2,0:T(8,128)(2,1)}), bf16[256,128,1,128]{3,1,2,0:T(8,128)(2,1)}) %all-gather.2.cloned.1.call-update) | async-done | bytes 8388624 | tf_op jit(solution)/shard_map/all_gather | solution.py:54
  103.8 4.2 %gather_fusion = bf16[48,128,128]{2,1,0:T(8,128)(2,1)S(1)} fusion(bf16[256,128,128]{2,1,0:T(8,128)(2,1)} %bitcast.194, s32[1024]{0:T(1024)S(1)} %pad_clamp_fusion), kind=kCustom, calls=%fused_computation | custom fusion | bytes 3145920 | tf_op jit(solution)/shard_map/jit(_take)/gather | solution.py:55
  108.3 1.9 fusion.36
  110.1 1.4 copy.66
  111.6 1.7 copy.65
  113.3 56.9 %while.10 = (s32[]{:T(128)}, bf16[12,4,32,1,64]{4,1,0,2,3:T(4,128)(2,1)}, s32[12,4,48]{2,1,0:T(4,128)}, bf16[12,4,32,1,64]{4,2,1,3,0:T(8,128)(2,1)}, bf16[48,128...) while((s32[]{:T(128)}, bf16[12,4,32,1,64]{4,1,0,2,3:T(4,128)(2,1)}, ...), condition=%wide.region_7.8_spmd, body=%wide.region_4.0_spmd.sunk | while | flops 210771904 | bytes 14258301 | solution.py:49
  113.3 0.7 fusion.55
  114.0 1.5 fusion.56
  115.5 0.9 fusion.57
  116.5 1.0 fusion.58
  118.1 0.7 fusion.55
  118.8 1.5 fusion.56
  120.2 0.9 fusion.57
  121.2 1.0 fusion.58
  123.5 1.5 fusion.56
  125.0 0.9 fusion.57
  125.9 1.0 fusion.58
  128.2 1.5 fusion.56
  129.7 0.9 fusion.57
  130.7 1.0 fusion.58
  133.0 1.5 fusion.56
  134.4 0.9 fusion.57
  135.4 1.0 fusion.58
  137.7 1.5 fusion.56
  139.2 0.9 fusion.57
  140.1 1.0 fusion.58
  142.4 1.5 fusion.56
  143.9 0.9 fusion.57
  144.9 1.0 fusion.58
  147.2 1.5 fusion.56
  148.7 0.9 fusion.57
  149.6 1.0 fusion.58
  151.9 1.5 fusion.56
  153.4 0.9 fusion.57
  154.4 1.0 fusion.58
  156.7 1.5 fusion.56
  158.2 0.9 fusion.57
  159.1 1.0 fusion.58
  161.4 1.5 fusion.56
  162.9 0.9 fusion.57
  163.9 1.0 fusion.58
  166.2 1.5 fusion.56
  167.6 0.9 fusion.57
  168.6 1.0 fusion.58
  170.2 1.4 reshape.180
  171.6 18.1 %all_to_all.79 = bf16[8,2,6144]{2,1,0:T(2,128)(2,1)S(1)} all-to-all(bf16[8,2,6144]{2,1,0:T(2,128)(2,1)S(1)} %reshape.180), channel_id=1, replica_groups=mesh['rows'=64,'cols'=8] {'cols'}, dimensions={0} | all-to-all | bytes 393216 | tf_op jit(solution)/shard_map/all_to_all | solution.py:103
  190.7 0.8 copy.69
  (94 shorter events, 21.4 us)
Async XLA Ops:
  6.5 3.1 %copy-start = (bf16[512,1536]{1,0:T(8,128)(2,1)S(1)}, bf16[512,1536]{1,0:T(8,128)(2,1)}, u32[]{:S(2)}) copy-start(bf16[512,1536]{1,0:T(8,128)(2,1)} %param.14) | copy-start | bytes 4718596
  6.5 97.3 %all-gather.2.cloned.1.call-start = ((), (), s32[]{:S(2)}) async-start(), calls=%async_computation.5 | async-start | bytes 8519680 | tf_op jit(solution)/shard_map/all_gather | solution.py:54
  12.1 20.8 %all-to-all-start.1 = ((bf16[8,2,6144]{2,1,0:T(2,128)(2,1)}), bf16[8,2,6144]{2,1,0:T(2,128)(2,1)S(1)}, u32[]{:S(2)}, u32[]{:S(2)}) async-start(bf16[8,2,6144]{2,1,0:T(2,128)(2,1)} %reshape.174), calls=%async_computation.1 | async-start | bytes 393216 | tf_op jit(solution)/shard_map/all_to_all | solution.py:89
  32.9 16.4 %all-to-all-start = ((bf16[48,4,8,128]{3,1,0,2:T(4,128)(2,1)}), bf16[48,4,8,128]{3,1,0,2:T(4,128)(2,1)S(1)}, u32[]{:S(2)}, u32[]{:S(2)}) async-start(bf16[48,4,8,128]{3,1,0,2:T(4,128)(2,1)} %pad_maximum_fusion), calls=%async_computation | async-start | bytes 786432 | tf_op jit(solution)/shard_map/all_to_all | solution.py:90
  50.8 15.1 %copy-start.1 = (bf16[48,4,512]{2,1,0:T(4,128)(2,1)S(1)}, bf16[48,4,512]{2,1,0:T(4,128)(2,1)}, u32[]{:S(2)}) copy-start(bf16[48,4,512]{2,1,0:T(4,128)(2,1)} %param.12) | copy-start | bytes 589828
  50.8 15.1 %copy-start.3 = (bf16[512,512]{1,0:T(8,128)(2,1)S(1)}, bf16[512,512]{1,0:T(8,128)(2,1)}, u32[]{:S(2)}) copy-start(bf16[512,512]{1,0:T(8,128)(2,1)} %param.15) | copy-start | bytes 1572868
  52.4 13.9 %copy-start.5 = (f32[512]{0:T(512)S(1)}, f32[512]{0:T(512)}, u32[]{:S(2)}) copy-start(f32[512]{0:T(512)} %param.16) | copy-start | bytes 6148
  65.7 7.3 %copy-start.6 = (s32[1,48]{1,0:T(1,128)S(1)}, s32[1,48]{1,0:T(1,128)}, u32[]{:S(2)}) copy-start(s32[1,48]{1,0:T(1,128)} %param.20) | copy-start | bytes 580
  69.3 13.1 %all-to-all-start.3 = ((bf16[8,2,6144]{2,1,0:T(2,128)(2,1)}), bf16[8,2,6144]{2,1,0:T(2,128)(2,1)S(1)}, u32[]{:S(2)}, u32[]{:S(2)}) async-start(bf16[8,2,6144]{2,1,0:T(2,128)(2,1)} %reshape.178), calls=%async_computation.3 | async-start | bytes 393216 | tf_op jit(solution)/shard_map/all_to_all | solution.py:101
  114.0 2.4 %copy-start.2 = (bf16[48,128,1,64]{1,3,0,2:T(8,128)(2,1)S(1)}, bf16[48,128,1,64]{1,3,0,2:T(8,128)(2,1)}, u32[]{:S(2)}) copy-start(bf16[48,128,1,64]{1,3,0,2:T(8,128)(2,1)} %get-tuple-element.141) | copy-start | bytes 2359300 | tf_op jit(solution)/shard_map/while
  118.8 2.4 %copy-start.2 = (bf16[48,128,1,64]{1,3,0,2:T(8,128)(2,1)S(1)}, bf16[48,128,1,64]{1,3,0,2:T(8,128)(2,1)}, u32[]{:S(2)}) copy-start(bf16[48,128,1,64]{1,3,0,2:T(8,128)(2,1)} %get-tuple-element.141) | copy-start | bytes 2359300 | tf_op jit(solution)/shard_map/while
  123.5 2.4 %copy-start.2 = (bf16[48,128,1,64]{1,3,0,2:T(8,128)(2,1)S(1)}, bf16[48,128,1,64]{1,3,0,2:T(8,128)(2,1)}, u32[]{:S(2)}) copy-start(bf16[48,128,1,64]{1,3,0,2:T(8,128)(2,1)} %get-tuple-element.141) | copy-start | bytes 2359300 | tf_op jit(solution)/shard_map/while
  128.2 2.4 %copy-start.2 = (bf16[48,128,1,64]{1,3,0,2:T(8,128)(2,1)S(1)}, bf16[48,128,1,64]{1,3,0,2:T(8,128)(2,1)}, u32[]{:S(2)}) copy-start(bf16[48,128,1,64]{1,3,0,2:T(8,128)(2,1)} %get-tuple-element.141) | copy-start | bytes 2359300 | tf_op jit(solution)/shard_map/while
  133.0 2.4 %copy-start.2 = (bf16[48,128,1,64]{1,3,0,2:T(8,128)(2,1)S(1)}, bf16[48,128,1,64]{1,3,0,2:T(8,128)(2,1)}, u32[]{:S(2)}) copy-start(bf16[48,128,1,64]{1,3,0,2:T(8,128)(2,1)} %get-tuple-element.141) | copy-start | bytes 2359300 | tf_op jit(solution)/shard_map/while
  137.7 2.4 %copy-start.2 = (bf16[48,128,1,64]{1,3,0,2:T(8,128)(2,1)S(1)}, bf16[48,128,1,64]{1,3,0,2:T(8,128)(2,1)}, u32[]{:S(2)}) copy-start(bf16[48,128,1,64]{1,3,0,2:T(8,128)(2,1)} %get-tuple-element.141) | copy-start | bytes 2359300 | tf_op jit(solution)/shard_map/while
  142.4 2.4 %copy-start.2 = (bf16[48,128,1,64]{1,3,0,2:T(8,128)(2,1)S(1)}, bf16[48,128,1,64]{1,3,0,2:T(8,128)(2,1)}, u32[]{:S(2)}) copy-start(bf16[48,128,1,64]{1,3,0,2:T(8,128)(2,1)} %get-tuple-element.141) | copy-start | bytes 2359300 | tf_op jit(solution)/shard_map/while
  147.2 2.4 %copy-start.2 = (bf16[48,128,1,64]{1,3,0,2:T(8,128)(2,1)S(1)}, bf16[48,128,1,64]{1,3,0,2:T(8,128)(2,1)}, u32[]{:S(2)}) copy-start(bf16[48,128,1,64]{1,3,0,2:T(8,128)(2,1)} %get-tuple-element.141) | copy-start | bytes 2359300 | tf_op jit(solution)/shard_map/while
  151.9 2.4 %copy-start.2 = (bf16[48,128,1,64]{1,3,0,2:T(8,128)(2,1)S(1)}, bf16[48,128,1,64]{1,3,0,2:T(8,128)(2,1)}, u32[]{:S(2)}) copy-start(bf16[48,128,1,64]{1,3,0,2:T(8,128)(2,1)} %get-tuple-element.141) | copy-start | bytes 2359300 | tf_op jit(solution)/shard_map/while
  156.7 2.4 %copy-start.2 = (bf16[48,128,1,64]{1,3,0,2:T(8,128)(2,1)S(1)}, bf16[48,128,1,64]{1,3,0,2:T(8,128)(2,1)}, u32[]{:S(2)}) copy-start(bf16[48,128,1,64]{1,3,0,2:T(8,128)(2,1)} %get-tuple-element.141) | copy-start | bytes 2359300 | tf_op jit(solution)/shard_map/while
  161.4 2.4 %copy-start.2 = (bf16[48,128,1,64]{1,3,0,2:T(8,128)(2,1)S(1)}, bf16[48,128,1,64]{1,3,0,2:T(8,128)(2,1)}, u32[]{:S(2)}) copy-start(bf16[48,128,1,64]{1,3,0,2:T(8,128)(2,1)} %get-tuple-element.141) | copy-start | bytes 2359300 | tf_op jit(solution)/shard_map/while
  166.2 2.4 %copy-start.2 = (bf16[48,128,1,64]{1,3,0,2:T(8,128)(2,1)S(1)}, bf16[48,128,1,64]{1,3,0,2:T(8,128)(2,1)}, u32[]{:S(2)}) copy-start(bf16[48,128,1,64]{1,3,0,2:T(8,128)(2,1)} %get-tuple-element.141) | copy-start | bytes 2359300 | tf_op jit(solution)/shard_map/while
  170.2 20.3 %copy-start.4 = (bf16[512,512]{1,0:T(8,128)(2,1)S(1)}, bf16[512,512]{1,0:T(8,128)(2,1)}, u32[]{:S(2)}) copy-start(bf16[512,512]{1,0:T(8,128)(2,1)} %param.18) | copy-start | bytes 1572868
Sparse Core Ops, SparseCore 0:
  10.7 93.0 all-gather.1
where the time goes:
time: 200 us; the launch traced here: 198 us
  waiting for transfers between devices  51.3 us (26%)
  matrix products  34.6 us (17%)
  blocking collectives  30.2 us (15%)
  local copies, waits for them, and re-layouts  27.5 us (14%)
  other arithmetic  23.4 us (12%)
  starting transfers between devices  17.3 us (9%)
  between operations  13.8 us (7%)
    all_gather x1, waiting for transfers between devices, fetch_all(): gathered = lax.all_gather(tile_kv, 'rows', axis=0, tiled=True)  20 us
    all_to_all x1, blocking collectives, shards(): lax.all_to_all(answer, 'cols', split_axis=1, concat_axis=2, tiled=True)  18.1 us
    dot_general x12, matrix products, one_block(): jnp.einsum('rchd,tkhd->rchtk', block_q, key_part, preferred_element_type=...  17.6 us
    all_to_all x1, waiting for transfers between devices, shards(): lax.all_to_all(keyvals, 'cols', split_axis=2, concat_axis=1, tiled=True)  12.4 us
    all_to_all x1, blocking collectives, shards(): lax.all_to_all(mixed_col, 'cols', split_axis=1, concat_axis=2, tiled=True)  12.2 us
    dot_general x12, matrix products, one_block(): jnp.einsum('rchtk,tkhd->rchd', tile_weights, val_part, preferred_element_...  11.6 us
    reduce_sum x12, other arithmetic, soft_weights(): jnp.sum(expo_vals, axis=axes, keepdims=True)  11.4 us
    all_to_all x1, starting transfers between devices, shards(): lax.all_to_all(queries, 'cols', split_axis=2, concat_axis=1, tiled=True)  10.3 us
  transfers between devices with their start and end apart: 4, of which 4 were waited for; matrix products, arithmetic and copies ran while one was open for 8% of the time, Pallas kernels for 0%

commit v1 on v0

--- a/solution.py
+++ b/solution.py
@@ -2,6 +2,18 @@
 import jax.numpy as jnp
 from jax import lax
 from jax.sharding import PartitionSpec as P
+
+
+def in_blocks(x, dim, size):
+    shape = x.shape
+    blocks = x.reshape(*shape[:dim], size, shape[dim] // size, *shape[dim + 1 :])
+    return jnp.moveaxis(blocks, dim, 0)
+
+
+def in_order(blocks, dim):
+    blocks = jnp.moveaxis(blocks, 0, dim)
+    shape = blocks.shape
+    return blocks.reshape(*shape[:dim], shape[dim] * shape[dim + 1], *shape[dim + 2 :])
 
 
 def rms_scale(values, gain_vec):
@@ -100,7 +112,14 @@
     )
     asked_h = lax.all_to_all(asked_q, "cols", split_axis=2, concat_axis=1, tiled=True)
     answer = tile_attend(asked_h, fetched, key_mask, head_size)
-    answer_back = lax.all_to_all(answer, "cols", split_axis=1, concat_axis=2, tiled=True)
+    devices, here = (lax.axis_size("cols"), lax.axis_index("cols"))
+    blocks = in_blocks(answer, 1, devices)
+    done = [blocks[here]]
+    for hop in range(1, devices):
+        sent = blocks[here ^ hop]
+        done.append(lax.ppermute(sent, "cols", [(i, i ^ hop) for i in range(devices)]))
+    blocks = jnp.stack(done)[here ^ jnp.arange(devices)]
+    answer_back = in_order(blocks, 2)
     final_out = residual + project(answer_back, w_tile_out).reshape(residual.shape)
     return final_out.astype(jnp.bfloat16)
 

time: 200 us -> 214 us (1.070)
  starting transfers between devices: 17.3 us -> 48.3 us
  blocking collectives: 30.2 us -> 0 us
  waiting for transfers between devices: 51.3 us -> 64.4 us
  matrix products: 34.6 us -> 41.9 us
  local copies, waits for them, and re-layouts: 27.5 us -> 20.7 us
    all_to_all x2 -> x0, blocking collectives: 30.2 us -> none  [the longest x1 18.1 us: shards(): lax.all_to_all(answer, 'cols', split_axis=1, concat_axis=2, tiled=True)]
    ppermute x0 -> x7, starting transfers between devices: none -> 27.6 us  [shards(): lax.ppermute(sent, 'cols', [(i, i ^ hop) for i in range(devices)])]
    all_to_all x0 -> x1, waiting for transfers between devices: none -> 9.65 us  [shards(): lax.all_to_all(mixed_col, 'cols', split_axis=1, concat_axis=2, tiled=True)]
    dynamic_update_slice x12 -> x0, local copies, waits for them, and re-layouts: 7.7 us -> none  [tile_attend(): answer = lax.map(one_block, (q_blocks, m_blocks))]
    dot_general x12, matrix products: 11.6 us -> 18.9 us  [one_block(): jnp.einsum('rchtk,tkhd->rchd', tile_weights, val_part, preferred_element_...]
    ppermute x0 -> x7, waiting for transfers between devices: none -> 5.17 us  [shards(): lax.ppermute(sent, 'cols', [(i, i ^ hop) for i in range(devices)])]
    all_to_all x0 -> x1, starting transfers between devices: none -> 3.39 us  [shards(): lax.all_to_all(mixed_col, 'cols', split_axis=1, concat_axis=2, tiled=True)]
    unnamed x21 -> x33, local copies, waits for them, and re-layouts: 4.96 us -> 4.13 us
  transfers between devices with their start and end apart: 4 -> 12, of which waited for: 4 -> 7; matrix products, arithmetic and copies ran while one was open for 8% -> 8% of each run, Pallas kernels for 0% -> 0%
where the time goes in v1:
time: 214 us; the launch traced here: 213 us
  waiting for transfers between devices  64.4 us (30%)
  starting transfers between devices  48.3 us (23%)
  matrix products  41.9 us (20%)
  other arithmetic  23.4 us (11%)
  local copies, waits for them, and re-layouts  20.7 us (10%)
  between operations  14 us (7%)
    ppermute x7, starting transfers between devices, shards(): lax.ppermute(sent, 'cols', [(i, i ^ hop) for i in range(devices)])  27.6 us
    dot_general x12, matrix products, one_block(): jnp.einsum('rchtk,tkhd->rchd', tile_weights, val_part, preferred_element_...  18.9 us
    all_gather x1, waiting for transfers between devices, fetch_all(): gathered = lax.all_gather(tile_kv, 'rows', axis=0, tiled=True)  18.4 us
    dot_general x12, matrix products, one_block(): jnp.einsum('rchd,tkhd->rchtk', block_q, key_part, preferred_element_type=...  17.6 us
    all_to_all x1, waiting for transfers between devices, shards(): lax.all_to_all(keyvals, 'cols', split_axis=2, concat_axis=1, tiled=True)  12.4 us
    reduce_sum x12, other arithmetic, soft_weights(): jnp.sum(expo_vals, axis=axes, keepdims=True)  11.4 us
    all_to_all x1, starting transfers between devices, shards(): lax.all_to_all(queries, 'cols', split_axis=2, concat_axis=1, tiled=True)  10.3 us
    all_to_all x1, waiting for transfers between devices, shards(): lax.all_to_all(mixed_col, 'cols', split_axis=1, concat_axis=2, tiled=True)  9.65 us
  transfers between devices with their start and end apart: 12, of which 7 were waited for; matrix products, arithmetic and copies ran while one was open for 8% of the time, Pallas kernels for 0%

profile of v1, /device:TPU:8, one launch (start us, length us, event | category | flops | bytes accessed | tf_op | source)
XLA Modules:
  0.0 213.1 jit_solution(3804164555816505858)
XLA Ops:
  7.3 1.1 fusion.33
  8.3 1.1 fusion.35
  11.1 1.0 reshape.209
  12.1 10.3 %all-to-all-start.1 = ((bf16[8,2,6144]{2,1,0:T(2,128)(2,1)}), bf16[8,2,6144]{2,1,0:T(2,128)(2,1)S(1)}, u32[]{:S(2)}, u32[]{:S(2)}) async-start(bf16[8,2,6144]{2,1,0:T(2,128)(2,1)} %reshape.209), calls=%async_computation.1 | async-start | bytes 393216 | tf_op jit(solution)/shard_map/all_to_all | solution.py:101
  22.8 1.3 pad_maximum_fusion
  24.1 8.8 %all-to-all-done.1 = bf16[8,2,6144]{2,1,0:T(2,128)(2,1)S(1)} async-done(((bf16[8,2,6144]{2,1,0:T(2,128)(2,1)}), bf16[8,2,6144]{2,1,0:T(2,128)(2,1)S(1)}, u32[]{:S(2)}, u32[]{:S(2)}) %all-to-all-start.1) | async-done | bytes 196640 | tf_op jit(solution)/shard_map/all_to_all | solution.py:101
  32.9 3.5 %all-to-all-start = ((bf16[48,4,8,128]{3,1,0,2:T(4,128)(2,1)}), bf16[48,4,8,128]{3,1,0,2:T(4,128)(2,1)S(1)}, u32[]{:S(2)}, u32[]{:S(2)}) async-start(bf16[48,4,8,128]{3,1,0,2:T(4,128)(2,1)} %pad_maximum_fusion), calls=%async_computation | async-start | bytes 786432 | tf_op jit(solution)/shard_map/all_to_all | solution.py:102
  37.0 12.4 %all-to-all-done = bf16[48,4,8,128]{3,1,0,2:T(4,128)(2,1)S(1)} async-done(((bf16[48,4,8,128]{3,1,0,2:T(4,128)(2,1)}), bf16[48,4,8,128]{3,1,0,2:T(4,128)(2,1)S(1)}, u32[]{:S(2)}, u32[]{:S(2)}) %all-to-all-start) | async-done | bytes 393248 | tf_op jit(solution)/shard_map/all_to_all | solution.py:102
  49.5 1.4 fusion.43
  50.9 1.6 fusion.29
  52.7 1.0 reshape.211
  53.7 3.4 %all-to-all-start.2 = ((bf16[8,2,6144]{2,1,0:T(2,128)(2,1)}), bf16[8,2,6144]{2,1,0:T(2,128)(2,1)S(1)}, u32[]{:S(2)}, u32[]{:S(2)}) async-start(bf16[8,2,6144]{2,1,0:T(2,128)(2,1)} %reshape.211), calls=%async_computation.2 | async-start | bytes 393216 | tf_op jit(solution)/shard_map/all_to_all | solution.py:105
  57.1 9.6 %all-to-all-done.2 = bf16[8,2,6144]{2,1,0:T(2,128)(2,1)S(1)} async-done(((bf16[8,2,6144]{2,1,0:T(2,128)(2,1)}), bf16[8,2,6144]{2,1,0:T(2,128)(2,1)S(1)}, u32[]{:S(2)}, u32[]{:S(2)}) %all-to-all-start.2) | async-done | bytes 196640 | tf_op jit(solution)/shard_map/all_to_all | solution.py:105
  68.3 1.3 convolution_convert_fusion.2
  70.0 1.0 reshape.213
  71.0 3.6 %all-to-all-start.3 = ((bf16[8,2,6144]{2,1,0:T(2,128)(2,1)}), bf16[8,2,6144]{2,1,0:T(2,128)(2,1)S(1)}, u32[]{:S(2)}, u32[]{:S(2)}) async-start(bf16[8,2,6144]{2,1,0:T(2,128)(2,1)} %reshape.213), calls=%async_computation.3 | async-start | bytes 393216 | tf_op jit(solution)/shard_map/all_to_all | solution.py:113
  74.7 9.4 %all-to-all-done.3 = bf16[8,2,6144]{2,1,0:T(2,128)(2,1)S(1)} async-done(((bf16[8,2,6144]{2,1,0:T(2,128)(2,1)}), bf16[8,2,6144]{2,1,0:T(2,128)(2,1)S(1)}, u32[]{:S(2)}, u32[]{:S(2)}) %all-to-all-start.3) | async-done | bytes 196640 | tf_op jit(solution)/shard_map/all_to_all | solution.py:113
  85.4 18.4 %all-gather.2.cloned.1.call-done = bf16[256,128,1,128]{3,1,2,0:T(8,128)(2,1)} async-done(((bf16[4,128,1,128]{3,1,2,0:T(8,128)(2,1)}), bf16[256,128,1,128]{3,1,2,0:T(8,128)(2,1)}) %all-gather.2.cloned.1.call-update) | async-done | bytes 8388624 | tf_op jit(solution)/shard_map/all_gather | solution.py:66
  103.8 4.2 %gather_fusion = bf16[48,128,128]{2,1,0:T(8,128)(2,1)S(1)} fusion(bf16[256,128,128]{2,1,0:T(8,128)(2,1)} %bitcast.243, s32[1024]{0:T(1024)S(1)} %pad_clamp_fusion.1), kind=kCustom, calls=%fused_computation | custom fusion | bytes 3145920 | tf_op jit(solution)/shard_map/jit(_take)/gather | solution.py:67
  108.2 1.9 fusion.41
  110.1 1.4 copy.101
  111.5 1.7 copy.100
  113.2 56.4 %while.10 = (s32[]{:T(128)}, bf16[12,4,32,1,64]{4,2,1,3,0:T(8,128)(2,1)}, s32[12,4,48]{2,1,0:T(4,128)}, bf16[12,4,32,1,64]{4,2,1,3,0:T(8,128)(2,1)}, bf16[48,128...) while((s32[]{:T(128)}, bf16[12,4,32,1,64]{4,2,1,3,0:T(8,128)(2,1)}, ...), condition=%wide.region_7.8_spmd, body=%wide.region_4.0_spmd.sunk | while | flops 210771904 | bytes 14225533 | solution.py:61
  113.9 1.5 fusion.61
  115.4 0.9 fusion.62
  116.4 1.6 fusion.63
  118.6 1.5 fusion.61
  120.1 0.9 fusion.62
  121.1 1.6 fusion.63
  123.3 1.5 fusion.61
  125.8 1.6 fusion.63
  128.0 1.5 fusion.61
  129.5 0.9 fusion.62
  130.5 1.6 fusion.63
  132.7 1.5 fusion.61
  134.2 0.9 fusion.62
  135.2 1.6 fusion.63
  137.4 1.5 fusion.61
  138.9 0.9 fusion.62
  139.9 1.6 fusion.63
  142.1 1.5 fusion.61
  143.6 0.9 fusion.62
  144.6 1.6 fusion.63
  146.8 1.5 fusion.61
  148.3 0.9 fusion.62
  149.3 1.6 fusion.63
  151.5 1.5 fusion.61
  154.0 1.6 fusion.63
  156.2 1.5 fusion.61
  158.7 1.6 fusion.63
  160.9 1.5 fusion.61
  163.4 1.6 fusion.63
  165.6 1.5 fusion.61
  168.1 1.6 fusion.63
  169.6 1.2 constant_dynamic-slice_fusion
  170.9 3.5 %collective-permute-start = (bf16[48,4,1,64]{3,0,1,2:T(8,128)(2,1)S(1)}, bf16[48,4,1,64]{3,0,1,2:T(8,128)(2,1)S(1)}, u32[]{:S(2)}, u32[]{:S(2)}) collective-permute-start(bf16[48,4,1,64]{3,0,1,2:T(8,128)(2,1)S(1)} %bitcast.250), channel_id=1, source_target_pairs={{0,1},{1,0},{2,3},{3,2},{4,5},{5,4},{6,7},{7,6},{8,9},{9,8},{10,11... | collective-permute-start | bytes 73736 | tf_op jit(solution)/shard_map/ppermute | solution.py:120
  174.4 4.6 %collective-permute-start.1 = (bf16[48,4,1,64]{3,0,1,2:T(8,128)(2,1)S(1)}, bf16[48,4,1,64]{3,0,1,2:T(8,128)(2,1)S(1)}, u32[]{:S(2)}, u32[]{:S(2)}) collective-permute-start(bf16[48,4,1,64]{3,0,1,2:T(8,128)(2,1)S(1)} %bitcast.249), channel_id=1, source_target_pairs={{0,2},{1,3},{2,0},{3,1},{4,6},{5,7},{6,4},{7,5},{8,10},{9,11},{10,... | collective-permute-start | bytes 73736 | tf_op jit(solution)/shard_map/ppermute | solution.py:120
  179.1 2.0 collective-permute-start.2
  181.0 8.0 %collective-permute-start.3 = (bf16[48,4,1,64]{3,0,1,2:T(8,128)(2,1)S(1)}, bf16[48,4,1,64]{3,0,1,2:T(8,128)(2,1)S(1)}, u32[]{:S(2)}, u32[]{:S(2)}) collective-permute-start(bf16[48,4,1,64]{3,0,1,2:T(8,128)(2,1)S(1)} %bitcast.245), channel_id=1, source_target_pairs={{0,4},{1,5},{2,6},{3,7},{4,0},{5,1},{6,2},{7,3},{8,12},{9,13},{10,... | collective-permute-start | bytes 73736 | tf_op jit(solution)/shard_map/ppermute | solution.py:120
  189.0 1.9 collective-permute-start.4
  191.0 5.7 %collective-permute-start.5 = (bf16[48,4,1,64]{3,0,1,2:T(8,128)(2,1)S(1)}, bf16[48,4,1,64]{3,0,1,2:T(8,128)(2,1)S(1)}, u32[]{:S(2)}, u32[]{:S(2)}) collective-permute-start(bf16[48,4,1,64]{3,0,1,2:T(8,128)(2,1)S(1)} %bitcast.248), channel_id=1, source_target_pairs={{0,6},{1,7},{2,4},{3,5},{4,2},{5,3},{6,0},{7,1},{8,14},{9,15},{10,... | collective-permute-start | bytes 73736 | tf_op jit(solution)/shard_map/ppermute | solution.py:120
  196.7 1.9 collective-permute-start.6
  198.8 1.0 collective-permute-done.5
  199.7 4.2 %collective-permute-done.6 = bf16[48,4,1,64]{3,0,1,2:T(8,128)(2,1)S(1)} collective-permute-done((bf16[48,4,1,64]{3,0,1,2:T(8,128)(2,1)S(1)}, bf16[48,4,1,64]{3,0,1,2:T(8,128)(2,1)S(1)}, u32[]{:S(2)}, u32[]{:S(2)}) %collective-permute-start.6) | collective-permute-done | bytes 24608 | tf_op jit(solution)/shard_map/ppermute | solution.py:120
  (113 shorter events, 22.5 us)
Async XLA Ops:
  6.5 3.1 %copy-start = (bf16[512,1536]{1,0:T(8,128)(2,1)S(1)}, bf16[512,1536]{1,0:T(8,128)(2,1)}, u32[]{:S(2)}) copy-start(bf16[512,1536]{1,0:T(8,128)(2,1)} %param.14) | copy-start | bytes 4718596
  6.5 97.2 %all-gather.2.cloned.1.call-start = ((), (), s32[]{:S(2)}) async-start(), calls=%async_computation.4 | async-start | bytes 8519680 | tf_op jit(solution)/shard_map/all_gather | solution.py:66
  12.1 20.8 %all-to-all-start.1 = ((bf16[8,2,6144]{2,1,0:T(2,128)(2,1)}), bf16[8,2,6144]{2,1,0:T(2,128)(2,1)S(1)}, u32[]{:S(2)}, u32[]{:S(2)}) async-start(bf16[8,2,6144]{2,1,0:T(2,128)(2,1)} %reshape.209), calls=%async_computation.1 | async-start | bytes 393216 | tf_op jit(solution)/shard_map/all_to_all | solution.py:101
  32.9 16.4 %all-to-all-start = ((bf16[48,4,8,128]{3,1,0,2:T(4,128)(2,1)}), bf16[48,4,8,128]{3,1,0,2:T(4,128)(2,1)S(1)}, u32[]{:S(2)}, u32[]{:S(2)}) async-start(bf16[48,4,8,128]{3,1,0,2:T(4,128)(2,1)} %pad_maximum_fusion), calls=%async_computation | async-start | bytes 786432 | tf_op jit(solution)/shard_map/all_to_all | solution.py:102
  49.5 7.6 %copy-start.6 = (s32[1,48]{1,0:T(1,128)S(1)}, s32[1,48]{1,0:T(1,128)}, u32[]{:S(2)}) copy-start(s32[1,48]{1,0:T(1,128)} %param.20) | copy-start | bytes 580
  50.9 16.7 %copy-start.1 = (bf16[48,4,512]{2,1,0:T(4,128)(2,1)S(1)}, bf16[48,4,512]{2,1,0:T(4,128)(2,1)}, u32[]{:S(2)}) copy-start(bf16[48,4,512]{2,1,0:T(4,128)(2,1)} %param.12) | copy-start | bytes 589828
  50.9 16.7 %copy-start.3 = (bf16[512,512]{1,0:T(8,128)(2,1)S(1)}, bf16[512,512]{1,0:T(8,128)(2,1)}, u32[]{:S(2)}) copy-start(bf16[512,512]{1,0:T(8,128)(2,1)} %param.15) | copy-start | bytes 1572868
  52.5 15.5 %copy-start.5 = (f32[512]{0:T(512)S(1)}, f32[512]{0:T(512)}, u32[]{:S(2)}) copy-start(f32[512]{0:T(512)} %param.16) | copy-start | bytes 6148
  53.7 13.1 %all-to-all-start.2 = ((bf16[8,2,6144]{2,1,0:T(2,128)(2,1)}), bf16[8,2,6144]{2,1,0:T(2,128)(2,1)S(1)}, u32[]{:S(2)}, u32[]{:S(2)}) async-start(bf16[8,2,6144]{2,1,0:T(2,128)(2,1)} %reshape.211), calls=%async_computation.2 | async-start | bytes 393216 | tf_op jit(solution)/shard_map/all_to_all | solution.py:105
  71.0 13.1 %all-to-all-start.3 = ((bf16[8,2,6144]{2,1,0:T(2,128)(2,1)}), bf16[8,2,6144]{2,1,0:T(2,128)(2,1)S(1)}, u32[]{:S(2)}, u32[]{:S(2)}) async-start(bf16[8,2,6144]{2,1,0:T(2,128)(2,1)} %reshape.213), calls=%async_computation.3 | async-start | bytes 393216 | tf_op jit(solution)/shard_map/all_to_all | solution.py:113
  113.9 2.4 %copy-start.2 = (bf16[48,128,1,64]{1,3,0,2:T(8,128)(2,1)S(1)}, bf16[48,128,1,64]{1,3,0,2:T(8,128)(2,1)}, u32[]{:S(2)}) copy-start(bf16[48,128,1,64]{1,3,0,2:T(8,128)(2,1)} %get-tuple-element.155) | copy-start | bytes 2359300 | tf_op jit(solution)/shard_map/while
  118.6 2.4 %copy-start.2 = (bf16[48,128,1,64]{1,3,0,2:T(8,128)(2,1)S(1)}, bf16[48,128,1,64]{1,3,0,2:T(8,128)(2,1)}, u32[]{:S(2)}) copy-start(bf16[48,128,1,64]{1,3,0,2:T(8,128)(2,1)} %get-tuple-element.155) | copy-start | bytes 2359300 | tf_op jit(solution)/shard_map/while
  123.3 2.4 %copy-start.2 = (bf16[48,128,1,64]{1,3,0,2:T(8,128)(2,1)S(1)}, bf16[48,128,1,64]{1,3,0,2:T(8,128)(2,1)}, u32[]{:S(2)}) copy-start(bf16[48,128,1,64]{1,3,0,2:T(8,128)(2,1)} %get-tuple-element.155) | copy-start | bytes 2359300 | tf_op jit(solution)/shard_map/while
  128.0 2.4 %copy-start.2 = (bf16[48,128,1,64]{1,3,0,2:T(8,128)(2,1)S(1)}, bf16[48,128,1,64]{1,3,0,2:T(8,128)(2,1)}, u32[]{:S(2)}) copy-start(bf16[48,128,1,64]{1,3,0,2:T(8,128)(2,1)} %get-tuple-element.155) | copy-start | bytes 2359300 | tf_op jit(solution)/shard_map/while
  132.7 2.4 %copy-start.2 = (bf16[48,128,1,64]{1,3,0,2:T(8,128)(2,1)S(1)}, bf16[48,128,1,64]{1,3,0,2:T(8,128)(2,1)}, u32[]{:S(2)}) copy-start(bf16[48,128,1,64]{1,3,0,2:T(8,128)(2,1)} %get-tuple-element.155) | copy-start | bytes 2359300 | tf_op jit(solution)/shard_map/while
  137.4 2.4 %copy-start.2 = (bf16[48,128,1,64]{1,3,0,2:T(8,128)(2,1)S(1)}, bf16[48,128,1,64]{1,3,0,2:T(8,128)(2,1)}, u32[]{:S(2)}) copy-start(bf16[48,128,1,64]{1,3,0,2:T(8,128)(2,1)} %get-tuple-element.155) | copy-start | bytes 2359300 | tf_op jit(solution)/shard_map/while
  142.1 2.4 %copy-start.2 = (bf16[48,128,1,64]{1,3,0,2:T(8,128)(2,1)S(1)}, bf16[48,128,1,64]{1,3,0,2:T(8,128)(2,1)}, u32[]{:S(2)}) copy-start(bf16[48,128,1,64]{1,3,0,2:T(8,128)(2,1)} %get-tuple-element.155) | copy-start | bytes 2359300 | tf_op jit(solution)/shard_map/while
  146.8 2.4 %copy-start.2 = (bf16[48,128,1,64]{1,3,0,2:T(8,128)(2,1)S(1)}, bf16[48,128,1,64]{1,3,0,2:T(8,128)(2,1)}, u32[]{:S(2)}) copy-start(bf16[48,128,1,64]{1,3,0,2:T(8,128)(2,1)} %get-tuple-element.155) | copy-start | bytes 2359300 | tf_op jit(solution)/shard_map/while
  151.5 2.4 %copy-start.2 = (bf16[48,128,1,64]{1,3,0,2:T(8,128)(2,1)S(1)}, bf16[48,128,1,64]{1,3,0,2:T(8,128)(2,1)}, u32[]{:S(2)}) copy-start(bf16[48,128,1,64]{1,3,0,2:T(8,128)(2,1)} %get-tuple-element.155) | copy-start | bytes 2359300 | tf_op jit(solution)/shard_map/while
  156.2 2.4 %copy-start.2 = (bf16[48,128,1,64]{1,3,0,2:T(8,128)(2,1)S(1)}, bf16[48,128,1,64]{1,3,0,2:T(8,128)(2,1)}, u32[]{:S(2)}) copy-start(bf16[48,128,1,64]{1,3,0,2:T(8,128)(2,1)} %get-tuple-element.155) | copy-start | bytes 2359300 | tf_op jit(solution)/shard_map/while
  160.9 2.4 %copy-start.2 = (bf16[48,128,1,64]{1,3,0,2:T(8,128)(2,1)S(1)}, bf16[48,128,1,64]{1,3,0,2:T(8,128)(2,1)}, u32[]{:S(2)}) copy-start(bf16[48,128,1,64]{1,3,0,2:T(8,128)(2,1)} %get-tuple-element.155) | copy-start | bytes 2359300 | tf_op jit(solution)/shard_map/while
  165.6 2.4 %copy-start.2 = (bf16[48,128,1,64]{1,3,0,2:T(8,128)(2,1)S(1)}, bf16[48,128,1,64]{1,3,0,2:T(8,128)(2,1)}, u32[]{:S(2)}) copy-start(bf16[48,128,1,64]{1,3,0,2:T(8,128)(2,1)} %get-tuple-element.155) | copy-start | bytes 2359300 | tf_op jit(solution)/shard_map/while
  169.6 35.5 %copy-start.4 = (bf16[512,512]{1,0:T(8,128)(2,1)S(1)}, bf16[512,512]{1,0:T(8,128)(2,1)}, u32[]{:S(2)}) copy-start(bf16[512,512]{1,0:T(8,128)(2,1)} %param.18) | copy-start | bytes 1572868
  170.9 20.1 %collective-permute-start = (bf16[48,4,1,64]{3,0,1,2:T(8,128)(2,1)S(1)}, bf16[48,4,1,64]{3,0,1,2:T(8,128)(2,1)S(1)}, u32[]{:S(2)}, u32[]{:S(2)}) collective-permute-start(bf16[48,4,1,64]{3,0,1,2:T(8,128)(2,1)S(1)} %bitcast.250), channel_id=1, source_target_pairs={{0,1},{1,0},{2,3},{3,2},{4,5},{5,4},{6,7},{7,6},{8,9},{9,8},{10,11... | collective-permute-start | bytes 73736 | tf_op jit(solution)/shard_map/ppermute | solution.py:120
  174.4 22.3 %collective-permute-start.1 = (bf16[48,4,1,64]{3,0,1,2:T(8,128)(2,1)S(1)}, bf16[48,4,1,64]{3,0,1,2:T(8,128)(2,1)S(1)}, u32[]{:S(2)}, u32[]{:S(2)}) collective-permute-start(bf16[48,4,1,64]{3,0,1,2:T(8,128)(2,1)S(1)} %bitcast.249), channel_id=1, source_target_pairs={{0,2},{1,3},{2,0},{3,1},{4,6},{5,7},{6,4},{7,5},{8,10},{9,11},{10,... | collective-permute-start | bytes 73736 | tf_op jit(solution)/shard_map/ppermute | solution.py:120
  179.1 19.6 %collective-permute-start.2 = (bf16[48,4,1,64]{3,0,1,2:T(8,128)(2,1)S(1)}, bf16[48,4,1,64]{3,0,1,2:T(8,128)(2,1)S(1)}, u32[]{:S(2)}, u32[]{:S(2)}) collective-permute-start(bf16[48,4,1,64]{3,0,1,2:T(8,128)(2,1)S(1)} %bitcast.246), channel_id=1, source_target_pairs={{0,3},{1,2},{2,1},{3,0},{4,7},{5,6},{6,5},{7,4},{8,11},{9,10},{10,... | collective-permute-start | bytes 73736 | tf_op jit(solution)/shard_map/ppermute | solution.py:120
  181.0 17.7 %collective-permute-start.3 = (bf16[48,4,1,64]{3,0,1,2:T(8,128)(2,1)S(1)}, bf16[48,4,1,64]{3,0,1,2:T(8,128)(2,1)S(1)}, u32[]{:S(2)}, u32[]{:S(2)}) collective-permute-start(bf16[48,4,1,64]{3,0,1,2:T(8,128)(2,1)S(1)} %bitcast.245), channel_id=1, source_target_pairs={{0,4},{1,5},{2,6},{3,7},{4,0},{5,1},{6,2},{7,3},{8,12},{9,13},{10,... | collective-permute-start | bytes 73736 | tf_op jit(solution)/shard_map/ppermute | solution.py:120
  189.0 9.7 %collective-permute-start.4 = (bf16[48,4,1,64]{3,0,1,2:T(8,128)(2,1)S(1)}, bf16[48,4,1,64]{3,0,1,2:T(8,128)(2,1)S(1)}, u32[]{:S(2)}, u32[]{:S(2)}) collective-permute-start(bf16[48,4,1,64]{3,0,1,2:T(8,128)(2,1)S(1)} %bitcast.244), channel_id=1, source_target_pairs={{0,5},{1,4},{2,7},{3,6},{4,1},{5,0},{6,3},{7,2},{8,13},{9,12},{10,... | collective-permute-start | bytes 73736 | tf_op jit(solution)/shard_map/ppermute | solution.py:120
  191.0 8.7 %collective-permute-start.5 = (bf16[48,4,1,64]{3,0,1,2:T(8,128)(2,1)S(1)}, bf16[48,4,1,64]{3,0,1,2:T(8,128)(2,1)S(1)}, u32[]{:S(2)}, u32[]{:S(2)}) collective-permute-start(bf16[48,4,1,64]{3,0,1,2:T(8,128)(2,1)S(1)} %bitcast.248), channel_id=1, source_target_pairs={{0,6},{1,7},{2,4},{3,5},{4,2},{5,3},{6,0},{7,1},{8,14},{9,15},{10,... | collective-permute-start | bytes 73736 | tf_op jit(solution)/shard_map/ppermute | solution.py:120
  196.7 7.2 %collective-permute-start.6 = (bf16[48,4,1,64]{3,0,1,2:T(8,128)(2,1)S(1)}, bf16[48,4,1,64]{3,0,1,2:T(8,128)(2,1)S(1)}, u32[]{:S(2)}, u32[]{:S(2)}) collective-permute-start(bf16[48,4,1,64]{3,0,1,2:T(8,128)(2,1)S(1)} %bitcast.247), channel_id=1, source_target_pairs={{0,7},{1,6},{2,5},{3,4},{4,3},{5,2},{6,1},{7,0},{8,15},{9,14},{10,... | collective-permute-start | bytes 73736 | tf_op jit(solution)/shard_map/ppermute | solution.py:120
Sparse Core Ops, SparseCore 0:
  10.7 93.0 all-gather.1
